TPU v7x, 256 devices: a whole 4x4x8 slice. The times are simulated.
256 devices in a mesh: tm: 8 (over x, core), row: 32 (over z, y).
Axes of the slice: x: 4, y: 4, z: 8, core: 2. Of those that a mesh axis runs over, the one named last changes fastest.
Arguments:
- pred_cov: bfloat16 [8, 1536, 1536], P('tm', 'row'), may hold values from -0.8 to 3.3, as said below
- cross: float32 [8, 1536, 1536], P('tm', 'row'), may hold values from -0.9 to 3.2
- filt_mean: float32 [8, 1536], P('tm', 'row'), may hold values from -6 to 6
- pred_mean: float32 [8, 1536], P('tm', 'row'), may hold values from -6 to 6
- next_smoothed: float32 [1536], P('row'), may hold values from -6 to 6
Outputs:
- smoothed: float32 [8, 1536], P('tm', 'row')
- gains: float32 [8, 1536, 1536], P('tm', 'row')
Inputs may be any that keep to these rules, and one draw needn't show every extreme that they name: `pred_cov`: each of the 8 matrices of size 1536 x 1536 is symmetric positive definite.
All inputs are finite; a program needn't handle non-finite values.
Results may differ from a plain program's by a relative error of at most 0.0003.
Values may be sent and summed in bfloat16 or wider, within the bound.
No kernel may reach another device: no remote copies, remote signals or barrier semaphores. Data moves between devices by JAX's collectives and lax.ppermute only.
A program may use at most 128 MiB of HBM per device.

v0:
```python
import jax
import jax.numpy as jnp
from jax import lax
from jax.sharding import PartitionSpec as P

finest = lax.Precision.HIGHEST


def from_behind(array, axis, by):
    peers = lax.axis_size(axis)
    pairs = [(i, i + by) for i in range(peers) if 0 <= i + by < peers]
    return lax.ppermute(array, axis, pairs)


def matvec(matrix, vector):
    return jnp.dot(matrix, vector, precision=finest, preferred_element_type=jnp.float32)


def per_device(pred_cov, cross, filt_mean, pred_mean, next_smoothed):
    whole_cov = lax.all_gather(pred_cov, "row", axis=1, tiled=True)
    cholesky_factor = jnp.linalg.cholesky(whole_cov[0].astype(jnp.float32))
    gain = jax.scipy.linalg.cho_solve((cholesky_factor, True), cross[0].T).T
    steps = lax.axis_size("tm")
    final = lax.axis_index("tm") == steps - 1
    mean_f = filt_mean[0]
    mean_p = pred_mean[0]

    def advance(turn, state):
        later = from_behind(state, "tm", -1)
        later = jnp.where(final, next_smoothed, later)
        dispersion = lax.all_gather(later - mean_p, "row", axis=0, tiled=True)
        return mean_f + matvec(gain, dispersion)

    smoothed = lax.fori_loop(0, steps, advance, jnp.zeros_like(mean_f))
    return (smoothed[None, :], gain[None, :, :])


def solution(mesh):
    in_specs = (
        P("tm", "row", None),
        P("tm", "row", None),
        P("tm", "row"),
        P("tm", "row"),
        P("row"),
    )
    out_specs = (P("tm", "row"), P("tm", "row", None))
    return jax.shard_map(
        per_device, mesh=mesh, in_specs=in_specs, out_specs=out_specs, check_vma=False
    )
```

profile of v0, /device:TPU:12, one launch (start us, length us, event | category | flops | bytes accessed | tf_op | source)
XLA Modules:
  0.0 1279.2 jit_solution(8773022271125293121)
XLA Ops:
  7.9 87.8 %all-gather.2.cloned.1.call-done = bf16[1,1536,1536]{2,1,0:T(8,128)(2,1)} async-done(((bf16[1,48,1536]{2,1,0:T(8,128)(2,1)}), bf16[1,1536,1536]{2,1,0:T(8,128)(2,1)}) %all-gather.2.cloned.1.call-update) | async-done | bytes 4718608 | tf_op jit(solution)/shard_map/all_gather | solution.py:20
  129.5 11.7 cholesky.341
  160.6 12.0 cholesky.362
  187.4 11.7 cholesky.385
  215.3 11.7 cholesky.715
  243.1 11.9 cholesky.734
  271.4 11.7 cholesky.754
  299.6 11.7 cholesky.774
  327.5 11.9 cholesky.794
  355.2 11.7 cholesky.814
  382.8 11.7 cholesky.834
  409.3 11.9 cholesky.854
  435.5 11.7 cholesky.872
  465.2 42.9 %while.12 = (s32[]{:T(128)}, f32[1536,1536]{1,0:T(8,128)}, s32[12,2]{0,1:T(2,128)S(1)}, f32[12,128,128]{2,1,0:T(8,128)}, s32[]{:T(128)}) while((s32[]{:T(128)}, f32[1536,1536]{1,0:T(8,128)}, s32[12,2]{0,1:T(2,128)S(1)}, f32[12,128,128]{2,1,0:T(8,128)}, s32[]{:T(128)}) %tuple.127), condition=%wide.while_cond, body=%wide.while_body.sunk | while | flops 2 | bytes 132705 | solution.py:22
  508.2 118.9 %custom-call.109 = f32[12,128,128]{1,2,0:T(8,128)S(1)} custom-call(f32[12,128,128]{2,1,0:T(8,128)} %get-tuple-element.47), custom_call_target="InvertDiagBlocksLowerTriangular" | custom-call | tf_op jit(solution)/shard_map/jit(_cho_solve)/triangular_solve | solution.py:22
  664.9 606.3 %while.13 = (s32[]{:T(128)}, f32[48]{0:T(128)S(1)}, pred[]{:T(512)}, f32[48]{0:T(128)S(1)}, f32[48]{0:T(128)S(1)}, /*index=5*/f32[48,1536]{1,0:T(8,128)S(1)}, f3...) while((s32[]{:T(128)}, f32[48]{0:T(128)S(1)}, ...), condition=%wide.region_25.26_spmd.clone, body=%wide.region_24.25_spmd.clone.sunk | while | flops 886470 | bytes 335592 | solution.py:34
  668.4 72.6 %all-reduce.4 = f32[1536]{0:T(1024)S(1)} all-reduce(f32[1536]{0:T(1024)S(1)} %fusion.208), channel_id=1, replica_groups=mesh['tm'=8,'row'=32] {'row'}, use_global_device_ids=true, to_apply=%add.1 | all-reduce | flops 1536 | bytes 12288 | tf_op jit(solution)/shard_map/while
  744.8 73.1 %all-reduce.4 = f32[1536]{0:T(1024)S(1)} all-reduce(f32[1536]{0:T(1024)S(1)} %fusion.208), channel_id=1, replica_groups=mesh['tm'=8,'row'=32] {'row'}, use_global_device_ids=true, to_apply=%add.1 | all-reduce | flops 1536 | bytes 12288 | tf_op jit(solution)/shard_map/while
  821.7 70.6 %all-reduce.4 = f32[1536]{0:T(1024)S(1)} all-reduce(f32[1536]{0:T(1024)S(1)} %fusion.208), channel_id=1, replica_groups=mesh['tm'=8,'row'=32] {'row'}, use_global_device_ids=true, to_apply=%add.1 | all-reduce | flops 1536 | bytes 12288 | tf_op jit(solution)/shard_map/while
  896.2 72.7 %all-reduce.4 = f32[1536]{0:T(1024)S(1)} all-reduce(f32[1536]{0:T(1024)S(1)} %fusion.208), channel_id=1, replica_groups=mesh['tm'=8,'row'=32] {'row'}, use_global_device_ids=true, to_apply=%add.1 | all-reduce | flops 1536 | bytes 12288 | tf_op jit(solution)/shard_map/while
  972.7 70.6 %all-reduce.4 = f32[1536]{0:T(1024)S(1)} all-reduce(f32[1536]{0:T(1024)S(1)} %fusion.208), channel_id=1, replica_groups=mesh['tm'=8,'row'=32] {'row'}, use_global_device_ids=true, to_apply=%add.1 | all-reduce | flops 1536 | bytes 12288 | tf_op jit(solution)/shard_map/while
  1047.2 72.7 %all-reduce.4 = f32[1536]{0:T(1024)S(1)} all-reduce(f32[1536]{0:T(1024)S(1)} %fusion.208), channel_id=1, replica_groups=mesh['tm'=8,'row'=32] {'row'}, use_global_device_ids=true, to_apply=%add.1 | all-reduce | flops 1536 | bytes 12288 | tf_op jit(solution)/shard_map/while
  1123.8 70.7 %all-reduce.4 = f32[1536]{0:T(1024)S(1)} all-reduce(f32[1536]{0:T(1024)S(1)} %fusion.208), channel_id=1, replica_groups=mesh['tm'=8,'row'=32] {'row'}, use_global_device_ids=true, to_apply=%add.1 | all-reduce | flops 1536 | bytes 12288 | tf_op jit(solution)/shard_map/while
  1198.2 72.6 %all-reduce.4 = f32[1536]{0:T(1024)S(1)} all-reduce(f32[1536]{0:T(1024)S(1)} %fusion.208), channel_id=1, replica_groups=mesh['tm'=8,'row'=32] {'row'}, use_global_device_ids=true, to_apply=%add.1 | all-reduce | flops 1536 | bytes 12288 | tf_op jit(solution)/shard_map/while
  (301 shorter events, 326.0 us)
Async XLA Ops:
  7.2 88.6 %all-gather.2.cloned.1.call-start = ((), (), s32[]{:S(2)}) async-start(), calls=%async_computation | async-start | bytes 4866048 | tf_op jit(solution)/shard_map/all_gather | solution.py:20
  125.9 3.6 copy-start
  456.7 170.3 %copy-start.2 = (f32[1,48,1536]{2,1,0:T(8,128)S(1)}, f32[1,48,1536]{2,1,0:T(8,128)}, u32[]{:S(2)}) copy-start(f32[1,48,1536]{2,1,0:T(8,128)} %param.8) | copy-start | bytes 884740
  631.2 33.7 %copy-start.3 = (f32[1,48]{1,0:T(1,128)S(1)}, f32[1,48]{1,0:T(1,128)}, u32[]{:S(2)}) copy-start(f32[1,48]{1,0:T(1,128)} %param.9) | copy-start | bytes 580
  631.2 33.7 %copy-start.4 = (f32[48]{0:T(128)S(1)}, f32[48]{0:T(128)}, u32[]{:S(2)}) copy-start(f32[48]{0:T(128)} %param.11) | copy-start | bytes 580
  631.2 33.7 %copy-start.5 = (f32[1,48]{1,0:T(1,128)S(1)}, f32[1,48]{1,0:T(1,128)}, u32[]{:S(2)}) copy-start(f32[1,48]{1,0:T(1,128)} %param.10) | copy-start | bytes 580
  631.2 33.7 %copy-start.6 = (u32[256]{0:T(256)S(1)}, u32[256]{0:T(256)}, u32[]{:S(2)}) copy-start(u32[256]{0:T(256)} %constant.815) | copy-start | bytes 3076
  664.9 3.3 collective-permute-start
  741.4 3.3 collective-permute-start
  818.3 3.3 collective-permute-start
  892.8 3.3 collective-permute-start
  969.3 3.3 collective-permute-start
  1043.8 3.3 collective-permute-start
  1120.3 3.3 collective-permute-start
  1194.8 3.3 collective-permute-start
  1271.2 0.7 copy-start.1
  1271.3 0.7 copy-start.7
Sparse Core Ops, SparseCore 0:
  10.6 85.1 all-gather.1
where the time goes:
time: 1290 us; the launch traced here: 1280 us
  blocking collectives  576 us (45%)
  other arithmetic  407 us (32%)
  matrix products  89.3 us (7%)
  waiting for transfers between devices  88.5 us (7%)
  local copies, waits for them, and re-layouts  74.1 us (6%)
  between operations  23.1 us (2%)
  starting transfers between devices  15.4 us (1%)
    while x8, blocking collectives  576 us
    another operation x46, other arithmetic, per_device(): cholesky_factor = jnp.linalg.cholesky(whole_cov[0].astype(jnp.float32))  264 us
    another operation x3, other arithmetic, per_device(): gain = jax.scipy.linalg.cho_solve((cholesky_factor, True), cross[0].T).T  127 us
    all_gather x1, waiting for transfers between devices, per_device(): whole_cov = lax.all_gather(pred_cov, 'row', axis=1, tiled=True)  87.8 us
    another operation x22, matrix products, per_device(): cholesky_factor = jnp.linalg.cholesky(whole_cov[0].astype(jnp.float32))  50.1 us
    another operation x36, local copies, waits for them, and re-layouts  42.9 us
    another operation x46, matrix products, per_device(): gain = jax.scipy.linalg.cho_solve((cholesky_factor, True), cross[0].T).T  36.7 us
  transfers between devices with their start and end apart: 9, of which 1 were waited for; matrix products, arithmetic and copies ran while one was open for 0% of the time, Pallas kernels for 0%

commit v1 on v0

--- a/solution.py
+++ b/solution.py
@@ -1,9 +1,21 @@
+import functools
 import jax
 import jax.numpy as jnp
 from jax import lax
 from jax.sharding import PartitionSpec as P
+from jax.lax import all_to_all, psum
 
 finest = lax.Precision.HIGHEST
+
+
+def view_outputs(my_data, dev_axis):
+    e_now = psum(1, dev_axis)
+    outer = jnp.stack(e_now * [my_data], axis=0)
+    tmp = all_to_all(outer, dev_axis, split_axis=0, concat_axis=0)
+    return jnp.concatenate(tmp, axis=1)
+
+
+state_the_group = functools.partial(view_outputs, dev_axis="row")
 
 
 def from_behind(array, axis, by):
@@ -17,7 +29,7 @@
 
 
 def per_device(pred_cov, cross, filt_mean, pred_mean, next_smoothed):
-    whole_cov = lax.all_gather(pred_cov, "row", axis=1, tiled=True)
+    whole_cov = state_the_group(pred_cov)
     cholesky_factor = jnp.linalg.cholesky(whole_cov[0].astype(jnp.float32))
     gain = jax.scipy.linalg.cho_solve((cholesky_factor, True), cross[0].T).T
     steps = lax.axis_size("tm")

time: 1290 us -> 1300 us (level)
  waiting for transfers between devices: 88.5 us -> 108 us
  between operations: 23.1 us -> 9.72 us
    all_to_all x0 -> x1, waiting for transfers between devices: none -> 108 us  [view_outputs(): tmp = all_to_all(outer, dev_axis, split_axis=0, concat_axis=0)]
    all_gather x1 -> x0, waiting for transfers between devices: 87.8 us -> none  [per_device(): whole_cov = lax.all_gather(pred_cov, 'row', axis=1, tiled=True)]
    another operation x36 -> x37, local copies, waits for them, and re-layouts: 42.9 us -> 46.5 us
where the time goes in v1:
time: 1300 us; the launch traced here: 1290 us
  blocking collectives  573 us (44%)
  other arithmetic  407 us (31%)
  waiting for transfers between devices  108 us (8%)
  matrix products  89.1 us (7%)
  local copies, waits for them, and re-layouts  71.1 us (5%)
  starting transfers between devices  27.2 us (2%)
    while x8, blocking collectives  573 us
    another operation x46, other arithmetic, per_device(): cholesky_factor = jnp.linalg.cholesky(whole_cov[0].astype(jnp.float32))  264 us
    another operation x3, other arithmetic, per_device(): gain = jax.scipy.linalg.cho_solve((cholesky_factor, True), cross[0].T).T  127 us
    all_to_all x1, waiting for transfers between devices, view_outputs(): tmp = all_to_all(outer, dev_axis, split_axis=0, concat_axis=0)  108 us
    another operation x22, matrix products, per_device(): cholesky_factor = jnp.linalg.cholesky(whole_cov[0].astype(jnp.float32))  50.1 us
    another operation x36, local copies, waits for them, and re-layouts  42.9 us
    another operation x46, matrix products, per_device(): gain = jax.scipy.linalg.cho_solve((cholesky_factor, True), cross[0].T).T  36.5 us
  transfers between devices with their start and end apart: 9, of which 1 were waited for; matrix products, arithmetic and copies ran while one was open for 0% of the time, Pallas kernels for 0%

profile of v1, /device:TPU:12, one launch (start us, length us, event | category | flops | bytes accessed | tf_op | source)
XLA Modules:
  0.0 1291.4 jit_solution(10172952149628062248)
XLA Ops:
  4.2 11.7 all-to-all-start
  16.0 108.3 %all-to-all-done = bf16[32,1,48,1536]{3,2,1,0:T(8,128)(2,1)} async-done(((bf16[32,1,48,1536]{3,2,1,0:T(8,128)(2,1)}), bf16[32,1,48,1536]{3,2,1,0:T(8,128)(2,1)}, u32[]{:S(2)}, u32[]{:S(2)}) %all-to-all-start) | async-done | bytes 4718624 | tf_op jit(solution)/shard_map/all_to_all | solution.py:14
  151.4 11.7 cholesky.341
  182.4 12.0 cholesky.362
  209.3 11.7 cholesky.385
  237.1 11.7 cholesky.715
  265.0 11.9 cholesky.734
  293.2 11.7 cholesky.754
  321.5 11.7 cholesky.774
  349.3 11.9 cholesky.794
  377.0 11.7 cholesky.814
  404.6 11.7 cholesky.834
  431.2 11.9 cholesky.854
  487.1 42.9 %while.12 = (s32[]{:T(128)}, f32[1536,1536]{1,0:T(8,128)}, s32[12,2]{0,1:T(2,128)S(1)}, f32[12,128,128]{2,1,0:T(8,128)}, s32[]{:T(128)}) while((s32[]{:T(128)}, f32[1536,1536]{1,0:T(8,128)}, s32[12,2]{0,1:T(2,128)S(1)}, f32[12,128,128]{2,1,0:T(8,128)}, s32[]{:T(128)}) %tuple.127), condition=%wide.while_cond, body=%wide.while_body.sunk | while | flops 2 | bytes 132705 | solution.py:34
  530.0 118.9 %custom-call.109 = f32[12,128,128]{1,2,0:T(8,128)S(1)} custom-call(f32[12,128,128]{2,1,0:T(8,128)} %get-tuple-element.47), custom_call_target="InvertDiagBlocksLowerTriangular" | custom-call | tf_op jit(solution)/shard_map/jit(_cho_solve)/triangular_solve | solution.py:34
  686.6 603.7 %while.13 = (s32[]{:T(128)}, f32[48]{0:T(128)S(1)}, pred[]{:T(512)}, f32[48]{0:T(128)S(1)}, f32[48]{0:T(128)S(1)}, /*index=5*/f32[48,1536]{1,0:T(8,128)S(1)}, f3...) while((s32[]{:T(128)}, f32[48]{0:T(128)S(1)}, ...), condition=%wide.region_25.26_spmd.clone, body=%wide.region_24.25_spmd.clone.sunk | while | flops 886470 | bytes 335592 | solution.py:46
  690.2 67.8 %all-reduce.4 = f32[1536]{0:T(1024)S(1)} all-reduce(f32[1536]{0:T(1024)S(1)} %fusion.208), channel_id=1, replica_groups=mesh['tm'=8,'row'=32] {'row'}, use_global_device_ids=true, to_apply=%add.1 | all-reduce | flops 1536 | bytes 12288 | tf_op jit(solution)/shard_map/while
  761.8 75.4 %all-reduce.4 = f32[1536]{0:T(1024)S(1)} all-reduce(f32[1536]{0:T(1024)S(1)} %fusion.208), channel_id=1, replica_groups=mesh['tm'=8,'row'=32] {'row'}, use_global_device_ids=true, to_apply=%add.1 | all-reduce | flops 1536 | bytes 12288 | tf_op jit(solution)/shard_map/while
  841.1 70.6 %all-reduce.4 = f32[1536]{0:T(1024)S(1)} all-reduce(f32[1536]{0:T(1024)S(1)} %fusion.208), channel_id=1, replica_groups=mesh['tm'=8,'row'=32] {'row'}, use_global_device_ids=true, to_apply=%add.1 | all-reduce | flops 1536 | bytes 12288 | tf_op jit(solution)/shard_map/while
  915.5 72.6 %all-reduce.4 = f32[1536]{0:T(1024)S(1)} all-reduce(f32[1536]{0:T(1024)S(1)} %fusion.208), channel_id=1, replica_groups=mesh['tm'=8,'row'=32] {'row'}, use_global_device_ids=true, to_apply=%add.1 | all-reduce | flops 1536 | bytes 12288 | tf_op jit(solution)/shard_map/while
  992.0 70.6 %all-reduce.4 = f32[1536]{0:T(1024)S(1)} all-reduce(f32[1536]{0:T(1024)S(1)} %fusion.208), channel_id=1, replica_groups=mesh['tm'=8,'row'=32] {'row'}, use_global_device_ids=true, to_apply=%add.1 | all-reduce | flops 1536 | bytes 12288 | tf_op jit(solution)/shard_map/while
  1066.4 72.6 %all-reduce.4 = f32[1536]{0:T(1024)S(1)} all-reduce(f32[1536]{0:T(1024)S(1)} %fusion.208), channel_id=1, replica_groups=mesh['tm'=8,'row'=32] {'row'}, use_global_device_ids=true, to_apply=%add.1 | all-reduce | flops 1536 | bytes 12288 | tf_op jit(solution)/shard_map/while
  1142.9 70.6 %all-reduce.4 = f32[1536]{0:T(1024)S(1)} all-reduce(f32[1536]{0:T(1024)S(1)} %fusion.208), channel_id=1, replica_groups=mesh['tm'=8,'row'=32] {'row'}, use_global_device_ids=true, to_apply=%add.1 | all-reduce | flops 1536 | bytes 12288 | tf_op jit(solution)/shard_map/while
  1217.3 72.6 %all-reduce.4 = f32[1536]{0:T(1024)S(1)} all-reduce(f32[1536]{0:T(1024)S(1)} %fusion.208), channel_id=1, replica_groups=mesh['tm'=8,'row'=32] {'row'}, use_global_device_ids=true, to_apply=%add.1 | all-reduce | flops 1536 | bytes 12288 | tf_op jit(solution)/shard_map/while
  (300 shorter events, 333.8 us)
Async XLA Ops:
  4.2 120.1 %all-to-all-start = ((bf16[32,1,48,1536]{3,2,1,0:T(8,128)(2,1)}), bf16[32,1,48,1536]{3,2,1,0:T(8,128)(2,1)}, u32[]{:S(2)}, u32[]{:S(2)}) async-start(bf16[32,1,48,1536]{3,2,1,0:T(8,128)(2,1)} %stack.2), calls=%async_computation | async-start | bytes 9437184 | tf_op jit(solution)/shard_map/all_to_all | solution.py:14
  147.7 3.6 copy-start
  478.6 170.3 %copy-start.2 = (f32[1,48,1536]{2,1,0:T(8,128)S(1)}, f32[1,48,1536]{2,1,0:T(8,128)}, u32[]{:S(2)}) copy-start(f32[1,48,1536]{2,1,0:T(8,128)} %param.8) | copy-start | bytes 884740
  653.0 33.5 %copy-start.3 = (f32[1,48]{1,0:T(1,128)S(1)}, f32[1,48]{1,0:T(1,128)}, u32[]{:S(2)}) copy-start(f32[1,48]{1,0:T(1,128)} %param.9) | copy-start | bytes 580
  653.1 33.5 %copy-start.4 = (f32[48]{0:T(128)S(1)}, f32[48]{0:T(128)}, u32[]{:S(2)}) copy-start(f32[48]{0:T(128)} %param.11) | copy-start | bytes 580
  653.1 33.5 %copy-start.5 = (f32[1,48]{1,0:T(1,128)S(1)}, f32[1,48]{1,0:T(1,128)}, u32[]{:S(2)}) copy-start(f32[1,48]{1,0:T(1,128)} %param.10) | copy-start | bytes 580
  653.1 33.5 %copy-start.6 = (u32[256]{0:T(256)S(1)}, u32[256]{0:T(256)}, u32[]{:S(2)}) copy-start(u32[256]{0:T(256)} %constant.815) | copy-start | bytes 3076
  686.6 3.4 collective-permute-start
  758.4 3.3 collective-permute-start
  837.6 3.3 collective-permute-start
  912.1 3.3 collective-permute-start
  988.5 3.3 collective-permute-start
  1063.0 3.3 collective-permute-start
  1139.4 3.3 collective-permute-start
  1213.9 3.3 collective-permute-start
  1290.3 0.7 copy-start.1
  1290.3 0.7 copy-start.7
